TPU v7x, 128 devices: a whole 4x4x4 slice. The times are simulated.
128 devices in a mesh: blk: 8 (over z, core), grp: 16 (over x, y).
Axes of the slice: x: 4, y: 4, z: 4, core: 2. Of those that a mesh axis runs over, the one named last changes fastest.
Arguments:
- user_prior: float32 [32768, 128], P(('blk', 'grp')), may hold values from -6 to 6
- item_factors: bfloat16 [524288, 128], P(('blk', 'grp')), may hold values from -0.375 to 0.375
- user_tiles: int32 [8192], P(('blk', 'grp')), may hold values from 0 to 31
- item_tiles: int32 [8192], P(('blk', 'grp')), may hold values from 0 to 4095, as said below
- counts: int32 [8192, 128, 128], P(('blk', 'grp')), may hold values from 0 to 20, as said below
Outputs:
- user_factors: float32 [32768, 128], P(('blk', 'grp'))
Inputs may be any that keep to these rules, and one draw needn't show every extreme that they name: `item_tiles`: item tile t is held by device t // 32 of blk+grp. The entries of one device name tiles of 32 different holders, exactly 2 entries for each holder that they name, in no particular order. In each device's 64 entries, those whose tile of counts has a nonzero value come before those whose tile is all zero; in every group along grp at least one device has all 64 entries of the first kind.
All inputs are finite; a program needn't handle non-finite values.
Results may differ from a plain program's by a relative error of at most 0.0003.
The roundings to bfloat16 on the way count: a program that leaves them out, or rounds other values in their place, can miss the bound.
Values may be sent and summed in bfloat16 or wider, within the bound.
A program may use at most 128 MiB of HBM per device.

v0:
```python
import jax
import jax.numpy as jnp
from jax import lax
from jax.sharding import PartitionSpec as P

ITERS = 3
ALPHA = 40.0
REG = 32.0
EPS = 1e-06


def fetch_tiles(item_factors, item_tiles, pairs, tile, rank):
    n_all = lax.axis_size(("blk", "grp"))
    tiles_held = item_factors.shape[0] // tile
    slots_each = max(2, pairs // n_all)
    owner = item_tiles // tiles_held
    local_slot = item_tiles % tiles_held
    position = jnp.arange(pairs, dtype=jnp.int32)
    earlier = (owner[None, :] == owner[:, None]) & (position[None, :] < position[:, None])
    order = jnp.sum(earlier.astype(jnp.int32), axis=1)
    requests = jnp.full((n_all, slots_each), -1, jnp.int32).at[owner, order].set(local_slot)
    wanted = lax.all_to_all(requests, ("blk", "grp"), split_axis=0, concat_axis=0, tiled=True)
    held = item_factors.reshape(tiles_held, tile, rank)
    picked = jnp.take(held, jnp.maximum(wanted, 0), axis=0)
    picked = jnp.where((wanted >= 0)[:, :, None, None], picked, jnp.zeros((), picked.dtype))
    arrived = lax.all_to_all(picked, ("blk", "grp"), split_axis=0, concat_axis=0, tiled=True)
    return arrived[owner, order]


def body(user_prior, item_factors, user_tiles, item_tiles, counts):
    pairs = counts.shape[0]
    tile = counts.shape[1]
    rank = item_factors.shape[1]
    n_grp = lax.axis_size("grp")
    own_rows = user_prior.shape[0]
    block_rows = own_rows * n_grp
    user_blocks = block_rows // tile
    span = min(32, pairs)
    gram_local = lax.dot_general(
        item_factors, item_factors, (((0,), (0,)), ((), ())), preferred_element_type=jnp.float32
    )
    gram = lax.psum(gram_local, ("blk", "grp"))
    pair_tiles = fetch_tiles(item_factors, item_tiles, pairs, tile, rank)
    live = jnp.sum(jnp.any(counts > 0, axis=(1, 2)).astype(jnp.int32))
    rounds = (live + span - 1) // span
    tile_ids = jnp.arange(user_blocks, dtype=jnp.int32)

    def accumulate(low_tiles, with_rhs):

        def one_round(index, totals):
            start = index * span
            users = lax.dynamic_slice_in_dim(user_tiles, start, span)
            factors = lax.dynamic_slice_in_dim(pair_tiles, start, span)
            counted = lax.dynamic_slice_in_dim(counts, start, span).astype(jnp.float32)
            selector = (tile_ids[:, None] == users[None, :]).astype(jnp.float32)
            users_low = jnp.take(low_tiles, users, axis=0)
            scores = jnp.einsum(
                "bur,bir->bui", users_low, factors, preferred_element_type=jnp.float32
            )
            scaled = (ALPHA * counted * scores).astype(jnp.bfloat16)
            back = jnp.einsum("bui,bir->bur", scaled, factors, preferred_element_type=jnp.float32)
            result = [
                totals[0]
                + jnp.einsum("tb,bur->tur", selector, back, precision=lax.Precision.HIGHEST)
            ]
            if with_rhs:
                confidence = jnp.where(counted > 0, 1.0 + ALPHA * counted, 0.0).astype(jnp.bfloat16)
                pulled = jnp.einsum(
                    "bui,bir->bur", confidence, factors, preferred_element_type=jnp.float32
                )
                result.append(
                    totals[1]
                    + jnp.einsum("tb,bur->tur", selector, pulled, precision=lax.Precision.HIGHEST)
                )
            return tuple(result)

        zeros = jnp.zeros((user_blocks, tile, rank), jnp.float32)
        start_state = (zeros, zeros) if with_rhs else (zeros,)
        totals = lax.fori_loop(0, rounds, one_round, start_state)
        return tuple((total.reshape(block_rows, rank) for total in totals))

    def gram_term(vectors):
        return jnp.dot(vectors, gram, precision=lax.Precision.HIGHEST) + REG * vectors

    def row_sum(left, right):
        return jnp.sum(left * right, axis=1, keepdims=True)

    whole = lax.all_gather(user_prior, "grp", axis=0, tiled=True)
    pair_part, rhs_part = accumulate(
        whole.astype(jnp.bfloat16).reshape(user_blocks, tile, rank), True
    )
    pair_total, rhs_total = lax.psum((pair_part, rhs_part), "grp")
    solution = whole
    residual = rhs_total - (gram_term(solution) + pair_total)
    direction = residual
    norm_now = row_sum(residual, residual)
    for step in range(ITERS):
        (pair_part,) = accumulate(
            direction.astype(jnp.bfloat16).reshape(user_blocks, tile, rank), False
        )
        image = gram_term(direction) + lax.psum(pair_part, "grp")
        alpha = norm_now / (row_sum(direction, image) + EPS)
        solution = solution + alpha * direction
        residual = residual - alpha * image
        fresh = row_sum(residual, residual)
        direction = residual + fresh / (norm_now + EPS) * direction
        norm_now = fresh
    return lax.dynamic_slice_in_dim(solution, lax.axis_index("grp") * own_rows, own_rows, 0)


def solution(mesh):
    in_specs = (
        P(("blk", "grp"), None),
        P(("blk", "grp"), None),
        P(("blk", "grp")),
        P(("blk", "grp")),
        P(("blk", "grp"), None, None),
    )
    out_specs = P(("blk", "grp"), None)
    return jax.shard_map(body, mesh=mesh, in_specs=in_specs, out_specs=out_specs, check_vma=False)
```

profile of v0, /device:TPU:0, one launch (start us, length us, event | category | flops | bytes accessed | tf_op | source)
XLA Modules:
  0.0 787.2 jit_solution(2010041510047153230)
XLA Ops:
  15.4 20.5 %all_to_all.14 = s32[128,1,2]{2,1,0:T(1,128)S(1)} all-to-all(s32[128,1,2]{2,1,0:T(1,128)S(1)} %copy.108), channel_id=1, replica_groups=mesh['blk'=8,'grp'=16] {'blk','grp'}, dimensions={0} | all-to-all | bytes 2048 | tf_op jit(solution)/shard_map/all_to_all | solution.py:22
  36.5 8.4 %gather_fusion.4 = bf16[256,128,128]{2,1,0:T(8,128)(2,1)} fusion(bf16[32,128,128]{2,1,0:T(8,128)(2,1)S(1)} %bitcast.108, s32[1024]{0:T(1024)S(1)} %pad_clamp_fusion.4), kind=kCustom, calls=%fused_computation.4 | custom fusion | bytes 16778240 | tf_op jit(solution)/shard_map/jit(_take)/gather | solution.py:24
  44.9 7.4 select_select_fusion
  52.3 6.1 all-to-all-start.1
  61.1 104.8 %all-gather.2.cloned.1.call-done = f32[4096,128]{0,1:T(8,128)} async-done(((f32[256,128]{0,1:T(8,128)}), f32[4096,128]{0,1:T(8,128)}) %all-gather.2.cloned.1.call-update) | async-done | bytes 2097168 | tf_op jit(solution)/shard_map/all_gather | solution.py:88
  176.5 18.2 %while.46 = (s32[]{:T(128)}, f32[32,128,128]{2,0,1:T(8,128)}, f32[32,128,128]{2,0,1:T(8,128)}, s32[]{:T(128)}, s32[64]{0:T(128)S(1)}, /*index=5*/s32[64,128,128]...) while((s32[]{:T(128)}, f32[32,128,128]{2,0,1:T(8,128)}, ...), condition=%wide.region_5.7_spmd.clone, body=%wide.region_4.6_spmd.clone.sunk | while | flops 812125440 | bytes 44048128 | solution.py:79
  182.9 6.1 fusion.187
  189.4 5.4 fusion.189
  198.3 4.6 copy.165
  206.3 4.6 copy.166
  211.2 58.5 %all-reduce.7.cloned.1.call-done = f32[128,128]{1,0:T(8,128)} async-done(((f32[128,128]{1,0:T(8,128)}), f32[128,128]{1,0:T(8,128)}) %all-reduce.7.cloned.1.call-update) | async-done | bytes 65552 | tf_op jit(solution)/shard_map/psum | solution.py:42
  269.7 105.7 %all-reduce.15.cloned.1.call-done = (f32[4096,128]{0,1:T(8,128)}, f32[4096,128]{0,1:T(8,128)}) async-done(((f32[4096,128]{0,1:T(8,128)}, f32[4096,128]{0,1:T(8,128)}), (f32[4096,128]{0,1:T(8,128)}, f32[4096,128]{0,1:T(8,128)})) %all-reduce.15.cloned.1.call-update) | async-done | bytes 4194320 | tf_op jit(solution)/shard_map/psum | solution.py:92
  375.5 7.0 fusion.133
  385.4 12.0 %while.47 = (s32[]{:T(128)}, f32[32,128,128]{2,0,1:T(8,128)}, s32[]{:T(128)}, s32[64]{0:T(128)S(1)}, s32[64,128,128]{2,1,0:T(8,128)}, /*index=5*/bf16[32,128,128...) while((s32[]{:T(128)}, f32[32,128,128]{2,0,1:T(8,128)}, ...), condition=%wide.region_11.13_spmd.clone, body=%wide.region_10.12_spmd.clone.sunk | while | flops 472910112 | bytes 15735391 | solution.py:79
  391.5 5.9 fusion.196
  405.9 102.4 %all-reduce.9.cloned.1.call-done = f32[4096,128]{0,1:T(8,128)} async-done(((f32[4096,128]{0,1:T(8,128)}), f32[4096,128]{0,1:T(8,128)}) %all-reduce.9.cloned.1.call-update) | async-done | bytes 2097168 | tf_op jit(solution)/shard_map/psum | solution.py:101
  508.3 5.5 multiply_reduce_fusion.3
  519.1 12.1 %while.48 = (s32[]{:T(128)}, f32[32,128,128]{2,0,1:T(8,128)}, s32[]{:T(128)}, s32[64]{0:T(128)S(1)}, s32[64,128,128]{2,1,0:T(8,128)}, /*index=5*/bf16[32,128,128...) while((s32[]{:T(128)}, f32[32,128,128]{2,0,1:T(8,128)}, ...), condition=%wide.region_16.18_spmd.clone, body=%wide.region_15.17_spmd.clone.sunk | while | flops 472910112 | bytes 15735391 | solution.py:79
  525.3 5.9 fusion.203
  539.5 101.9 %all-reduce.11.cloned.1.call-done = f32[4096,128]{0,1:T(8,128)} async-done(((f32[4096,128]{0,1:T(8,128)}), f32[4096,128]{0,1:T(8,128)}) %all-reduce.11.cloned.1.call-update) | async-done | bytes 2097168 | tf_op jit(solution)/shard_map/psum | solution.py:101
  641.4 5.3 multiply_reduce_fusion.1
  653.1 12.3 %while.49 = (s32[]{:T(128)}, f32[32,128,128]{2,0,1:T(8,128)}, s32[]{:T(128)}, s32[64]{0:T(128)S(1)}, s32[64,128,128]{2,1,0:T(8,128)}, /*index=5*/bf16[32,128,128...) while((s32[]{:T(128)}, f32[32,128,128]{2,0,1:T(8,128)}, ...), condition=%wide.region_21.23_spmd.clone, body=%wide.region_20.22_spmd.clone.sunk | while | flops 472910112 | bytes 15735391 | solution.py:79
  659.3 5.9 fusion.210
  671.3 102.4 %all-reduce.13.cloned.1.call-done = f32[4096,128]{0,1:T(8,128)} async-done(((f32[4096,128]{0,1:T(8,128)}), f32[4096,128]{0,1:T(8,128)}) %all-reduce.13.cloned.1.call-update) | async-done | bytes 2097168 | tf_op jit(solution)/shard_map/psum | solution.py:101
  (109 shorter events, 96.5 us)
Async XLA Ops:
  7.4 29.1 %copy-start = (bf16[4096,128]{1,0:T(8,128)(2,1)S(1)}, bf16[4096,128]{1,0:T(8,128)(2,1)}, u32[]{:S(2)}) copy-start(bf16[4096,128]{1,0:T(8,128)(2,1)} %param.16) | copy-start | bytes 3145732
  7.4 3.5 copy-start.11
  52.3 6.1 copy-start.10
  52.3 116.7 %all-to-all-start.1 = ((bf16[128,2,128,128]{3,2,1,0:T(8,128)(2,1)}), bf16[128,2,128,128]{3,2,1,0:T(8,128)(2,1)}, u32[]{:S(2)}, u32[]{:S(2)}) async-start(bf16[128,2,128,128]{3,2,1,0:T(8,128)(2,1)} %select_select_fusion), calls=%async_computation.1 | async-start | bytes 16777216 | tf_op jit(solution)/shard_map/all_to_all | solution.py:26
  58.4 107.5 %all-gather.2.cloned.1.call-start = ((), (), s32[]{:S(2)}) async-start(), calls=%async_computation.2 | async-start | bytes 2228224 | tf_op jit(solution)/shard_map/all_gather | solution.py:88
  59.2 210.5 %all-reduce.7.cloned.1.call-start = ((), (), s32[]{:S(2)}) async-start(), calls=%async_computation.3 | async-start | bytes 131072 | tf_op jit(solution)/shard_map/psum | solution.py:42
  60.4 315.1 %all-reduce.15.cloned.1.call-start = ((), (), s32[]{:S(2)}) async-start(), calls=%async_computation.7 | async-start | bytes 8388608 | tf_op jit(solution)/shard_map/psum | solution.py:92
  173.3 3.2 copy-start.9
  182.9 6.1 copy-start.2
  210.9 297.3 %all-reduce.9.cloned.1.call-start = ((), (), s32[]{:S(2)}) async-start(), calls=%async_computation.4 | async-start | bytes 4194304 | tf_op jit(solution)/shard_map/psum | solution.py:101
  405.4 102.9 %copy-start.8 = (f32[128,128]{1,0:T(8,128)S(1)}, f32[128,128]{1,0:T(8,128)}, u32[]{:S(2)}) copy-start(f32[128,128]{1,0:T(8,128)} %all-reduce.7.cloned.1.call-done) | copy-start | bytes 196612
  405.4 236.0 %all-reduce.11.cloned.1.call-start = ((), (), s32[]{:S(2)}) async-start(), calls=%async_computation.5 | async-start | bytes 4194304 | tf_op jit(solution)/shard_map/psum | solution.py:101
  508.3 5.5 copy-start.3
  514.2 2.0 copy-start.4
  539.3 234.4 %all-reduce.13.cloned.1.call-start = ((), (), s32[]{:S(2)}) async-start(), calls=%async_computation.6 | async-start | bytes 4194304 | tf_op jit(solution)/shard_map/psum | solution.py:101
  641.4 5.4 copy-start.5
  646.7 1.6 copy-start.6
  671.1 102.6 %copy-start.7 = (f32[4096,128]{0,1:T(8,128)S(1)}, f32[4096,128]{0,1:T(8,128)}, u32[]{:S(2)}) copy-start(f32[4096,128]{0,1:T(8,128)} %get-tuple-element.504) | copy-start | bytes 6291460
  773.7 5.9 copy-start.1
Sparse Core Ops, SparseCore 0:
  61.3 104.5 all-gather.1
  405.5 102.6 all-reduce.8
  671.2 102.3 all-reduce.12
Sparse Core Ops, SparseCore 1:
  64.5 205.2 all-reduce.6
  273.0 102.4 all-reduce.14
  539.3 102.0 all-reduce.10
where the time goes:
time: 795 us; the launch traced here: 787 us
  waiting for transfers between devices  576 us (72%)
  local copies, waits for them, and re-layouts  78.9 us (10%)
  matrix products  69 us (9%)
  blocking collectives  20.5 us (3%)
  other arithmetic  19.5 us (2%)
  between operations  16 us (2%)
    psum x3, waiting for transfers between devices, body(): image = gram_term(direction) + lax.psum(pair_part, 'grp')  307 us
    psum x1, waiting for transfers between devices, body(): pair_total, rhs_total = lax.psum((pair_part, rhs_part), 'grp')  106 us
    all_gather x1, waiting for transfers between devices, body(): whole = lax.all_gather(user_prior, 'grp', axis=0, tiled=True)  105 us
    psum x1, waiting for transfers between devices, body(): gram = lax.psum(gram_local, ('blk', 'grp'))  58.5 us
    unnamed x32, local copies, waits for them, and re-layouts  28.6 us
    dot_general x4, matrix products, one_round(): jnp.einsum('tb,bur->tur', selector, back, precision=lax.Precision.HIGHEST)  23.8 us
    dot_general x4, matrix products, gram_term(): jnp.dot(vectors, gram, precision=lax.Precision.HIGHEST) + REG * vectors  21.8 us
    all_to_all x1, blocking collectives, fetch_tiles(): lax.all_to_all(requests, ('blk', 'grp'), split_axis=0, concat_axis=0, til...  20.5 us
  transfers between devices with their start and end apart: 7, of which 6 were waited for; matrix products, arithmetic and copies ran while one was open for 6% of the time, Pallas kernels for 0%

commit v1 on v0

--- a/solution.py
+++ b/solution.py
@@ -28,6 +28,11 @@
 
 
 def body(user_prior, item_factors, user_tiles, item_tiles, counts):
+
+    def group_cubes_up(along_axis, mesh_dim, original):
+        v1 = lax.psum(lax.psum(original, along_axis), mesh_dim)
+        return v1
+
     pairs = counts.shape[0]
     tile = counts.shape[1]
     rank = item_factors.shape[1]
@@ -39,7 +44,7 @@
     gram_local = lax.dot_general(
         item_factors, item_factors, (((0,), (0,)), ((), ())), preferred_element_type=jnp.float32
     )
-    gram = lax.psum(gram_local, ("blk", "grp"))
+    gram = group_cubes_up("blk", "grp", gram_local)
     pair_tiles = fetch_tiles(item_factors, item_tiles, pairs, tile, rank)
     live = jnp.sum(jnp.any(counts > 0, axis=(1, 2)).astype(jnp.int32))
     rounds = (live + span - 1) // span

time: 795 us -> 754 us (0.948)
  waiting for transfers between devices: 576 us -> 534 us
    psum x1, waiting for transfers between devices: 58.5 us -> 0.01 us  [group_cubes_up(): v1 = lax.psum(lax.psum(original, along_axis), mesh_dim)]
    psum x1, waiting for transfers between devices: 106 us -> 122 us  [body(): pair_total, rhs_total = lax.psum((pair_part, rhs_part), 'grp')]
    unnamed x32 -> x30, local copies, waits for them, and re-layouts: 28.6 us -> 28.6 us
  transfers between devices with their start and end apart: 7 -> 7, of which waited for: 6 -> 5; matrix products, arithmetic and copies ran while one was open for 6% -> 6% of each run, Pallas kernels for 0% -> 0%
where the time goes in v1:
time: 754 us; the launch traced here: 746 us
  waiting for transfers between devices  534 us (71%)
  local copies, waits for them, and re-layouts  78.8 us (10%)
  matrix products  70.2 us (9%)
  blocking collectives  20.5 us (3%)
  other arithmetic  19.5 us (3%)
  between operations  15.6 us (2%)
    psum x3, waiting for transfers between devices, body(): image = gram_term(direction) + lax.psum(pair_part, 'grp')  307 us
    psum x1, waiting for transfers between devices, body(): pair_total, rhs_total = lax.psum((pair_part, rhs_part), 'grp')  122 us
    all_gather x1, waiting for transfers between devices, body(): whole = lax.all_gather(user_prior, 'grp', axis=0, tiled=True)  105 us
    unnamed x30, local copies, waits for them, and re-layouts  28.6 us
    dot_general x4, matrix products, one_round(): jnp.einsum('tb,bur->tur', selector, back, precision=lax.Precision.HIGHEST)  23.8 us
    dot_general x4, matrix products, gram_term(): jnp.dot(vectors, gram, precision=lax.Precision.HIGHEST) + REG * vectors  23.1 us
    all_to_all x1, blocking collectives, fetch_tiles(): lax.all_to_all(requests, ('blk', 'grp'), split_axis=0, concat_axis=0, til...  20.5 us
    while x5, local copies, waits for them, and re-layouts, accumulate(): totals = lax.fori_loop(0, rounds, one_round, start_state)  16.4 us
  transfers between devices with their start and end apart: 7, of which 5 were waited for; matrix products, arithmetic and copies ran while one was open for 6% of the time, Pallas kernels for 0%

profile of v1, /device:TPU:0, one launch (start us, length us, event | category | flops | bytes accessed | tf_op | source)
XLA Modules:
  0.0 746.4 jit_solution(12308487806630761720)
XLA Ops:
  15.3 20.5 %all_to_all.14 = s32[128,1,2]{2,1,0:T(1,128)S(1)} all-to-all(s32[128,1,2]{2,1,0:T(1,128)S(1)} %copy.108), channel_id=1, replica_groups=mesh['blk'=8,'grp'=16] {'blk','grp'}, dimensions={0} | all-to-all | bytes 2048 | tf_op jit(solution)/shard_map/all_to_all | solution.py:22
  36.4 8.4 %gather_fusion.4 = bf16[256,128,128]{2,1,0:T(8,128)(2,1)} fusion(bf16[32,128,128]{2,1,0:T(8,128)(2,1)S(1)} %bitcast.108, s32[1024]{0:T(1024)S(1)} %pad_clamp_fusion.4), kind=kCustom, calls=%fused_computation.4 | custom fusion | bytes 16778240 | tf_op jit(solution)/shard_map/jit(_take)/gather | solution.py:24
  44.8 7.4 select_select_fusion
  52.2 6.1 all-to-all-start.1
  60.9 105.2 %all-gather.2.cloned.1.call-done = f32[4096,128]{0,1:T(8,128)} async-done(((f32[256,128]{0,1:T(8,128)}), f32[4096,128]{0,1:T(8,128)}) %all-gather.2.cloned.1.call-update) | async-done | bytes 2097168 | tf_op jit(solution)/shard_map/all_gather | solution.py:93
  176.7 18.2 %while.46 = (s32[]{:T(128)}, f32[32,128,128]{2,0,1:T(8,128)}, f32[32,128,128]{2,0,1:T(8,128)}, s32[]{:T(128)}, s32[64]{0:T(128)S(1)}, /*index=5*/s32[64,128,128]...) while((s32[]{:T(128)}, f32[32,128,128]{2,0,1:T(8,128)}, ...), condition=%wide.region_5.7_spmd.clone, body=%wide.region_4.6_spmd.clone.sunk | while | flops 812125440 | bytes 44048128 | solution.py:84
  183.1 6.1 fusion.187
  189.6 5.4 fusion.189
  198.4 4.6 copy.165
  211.3 121.8 %all-reduce.15.cloned.1.call-done = (f32[4096,128]{0,1:T(8,128)}, f32[4096,128]{0,1:T(8,128)}, f32[128,128]{1,0:T(8,128)}) async-done(((f32[4096,128]{0,1:T(8,128)}, f32[4096,128]{0,1:T(8,128)}, f32[128,128]{1,0:T(8,128)}), (f32[4096,128]{0,1:T(8,128)}, f32[4096,128]{0,1:T(8,128)}, f32[128,128]{1,0:T(8,128)})) %all-reduce.15.cloned.1.call-update) | async-done | bytes 4259856 | tf_op jit(solution)/shard_map/psum | solution.py:97
  333.1 7.0 fusion.133
  343.0 12.0 %while.47 = (s32[]{:T(128)}, f32[32,128,128]{2,0,1:T(8,128)}, s32[]{:T(128)}, s32[64]{0:T(128)S(1)}, s32[64,128,128]{2,1,0:T(8,128)}, /*index=5*/bf16[32,128,128...) while((s32[]{:T(128)}, f32[32,128,128]{2,0,1:T(8,128)}, ...), condition=%wide.region_12.14_spmd.clone, body=%wide.region_11.13_spmd.clone.sunk | while | flops 472910112 | bytes 15735391 | solution.py:84
  349.2 5.9 fusion.196
  363.3 102.4 %all-reduce.9.cloned.1.call-done = f32[4096,128]{0,1:T(8,128)} async-done(((f32[4096,128]{0,1:T(8,128)}), f32[4096,128]{0,1:T(8,128)}) %all-reduce.9.cloned.1.call-update) | async-done | bytes 2097168 | tf_op jit(solution)/shard_map/psum | solution.py:106
  465.8 5.5 multiply_reduce_fusion.3
  476.6 12.1 %while.48 = (s32[]{:T(128)}, f32[32,128,128]{2,0,1:T(8,128)}, s32[]{:T(128)}, s32[64]{0:T(128)S(1)}, s32[64,128,128]{2,1,0:T(8,128)}, /*index=5*/bf16[32,128,128...) while((s32[]{:T(128)}, f32[32,128,128]{2,0,1:T(8,128)}, ...), condition=%wide.region_17.19_spmd.clone, body=%wide.region_16.18_spmd.clone.sunk | while | flops 472910112 | bytes 15735391 | solution.py:84
  482.8 5.9 fusion.203
  492.1 4.6 copy.163
  497.2 102.2 %all-reduce.11.cloned.1.call-done = f32[4096,128]{0,1:T(8,128)} async-done(((f32[4096,128]{0,1:T(8,128)}), f32[4096,128]{0,1:T(8,128)}) %all-reduce.11.cloned.1.call-update) | async-done | bytes 2097168 | tf_op jit(solution)/shard_map/psum | solution.py:106
  599.4 5.3 multiply_reduce_fusion.1
  611.2 12.3 %while.49 = (s32[]{:T(128)}, f32[32,128,128]{2,0,1:T(8,128)}, s32[]{:T(128)}, s32[64]{0:T(128)S(1)}, s32[64,128,128]{2,1,0:T(8,128)}, /*index=5*/bf16[32,128,128...) while((s32[]{:T(128)}, f32[32,128,128]{2,0,1:T(8,128)}, ...), condition=%wide.region_22.24_spmd.clone, body=%wide.region_21.23_spmd.clone.sunk | while | flops 472910112 | bytes 15735391 | solution.py:84
  617.3 5.9 fusion.210
  629.3 102.5 %all-reduce.13.cloned.1.call-done = f32[4096,128]{0,1:T(8,128)} async-done(((f32[4096,128]{0,1:T(8,128)}), f32[4096,128]{0,1:T(8,128)}) %all-reduce.13.cloned.1.call-update) | async-done | bytes 2097168 | tf_op jit(solution)/shard_map/psum | solution.py:106
  731.8 5.2 fusion.123
  (107 shorter events, 92.5 us)
Async XLA Ops:
  7.4 29.0 %copy-start = (bf16[4096,128]{1,0:T(8,128)(2,1)S(1)}, bf16[4096,128]{1,0:T(8,128)(2,1)}, u32[]{:S(2)}) copy-start(bf16[4096,128]{1,0:T(8,128)(2,1)} %param.16) | copy-start | bytes 3145732
  7.4 3.5 copy-start.10
  52.2 6.1 copy-start.9
  52.2 117.0 %all-to-all-start.1 = ((bf16[128,2,128,128]{3,2,1,0:T(8,128)(2,1)}), bf16[128,2,128,128]{3,2,1,0:T(8,128)(2,1)}, u32[]{:S(2)}, u32[]{:S(2)}) async-start(bf16[128,2,128,128]{3,2,1,0:T(8,128)(2,1)} %select_select_fusion), calls=%async_computation.1 | async-start | bytes 16777216 | tf_op jit(solution)/shard_map/all_to_all | solution.py:26
  58.3 107.8 %all-gather.2.cloned.1.call-start = ((), (), s32[]{:S(2)}) async-start(), calls=%async_computation.2 | async-start | bytes 2228224 | tf_op jit(solution)/shard_map/all_gather | solution.py:93
  59.1 151.9 %all-reduce.7.cloned.1.call-start = ((), (), s32[]{:S(2)}) async-start(), calls=%async_computation.3 | async-start | bytes 131072 | tf_op jit(solution)/shard_map/psum | solution.py:33
  60.3 272.8 %all-reduce.15.cloned.1.call-start = ((), (), s32[]{:S(2)}) async-start(), calls=%async_computation.7 | async-start | bytes 8519680 | tf_op jit(solution)/shard_map/psum | solution.py:97
  173.5 3.2 copy-start.8
  183.1 6.1 copy-start.2
  211.0 254.7 %all-reduce.9.cloned.1.call-start = ((), (), s32[]{:S(2)}) async-start(), calls=%async_computation.4 | async-start | bytes 4194304 | tf_op jit(solution)/shard_map/psum | solution.py:106
  363.0 102.7 %copy-start.7 = (f32[128,128]{1,0:T(8,128)S(1)}, f32[128,128]{1,0:T(8,128)}, u32[]{:S(2)}) copy-start(f32[128,128]{1,0:T(8,128)} %get-tuple-element.495) | copy-start | bytes 196612
  363.0 236.4 %all-reduce.11.cloned.1.call-start = ((), (), s32[]{:S(2)}) async-start(), calls=%async_computation.5 | async-start | bytes 4194304 | tf_op jit(solution)/shard_map/psum | solution.py:106
  465.8 5.5 copy-start.3
  471.7 2.0 copy-start.4
  496.7 235.1 %all-reduce.13.cloned.1.call-start = ((), (), s32[]{:S(2)}) async-start(), calls=%async_computation.6 | async-start | bytes 4194304 | tf_op jit(solution)/shard_map/psum | solution.py:106
  599.4 5.4 copy-start.5
  604.8 1.6 copy-start.6
  731.8 7.2 copy-start.1
Sparse Core Ops, SparseCore 0:
  61.2 104.8 all-gather.1
  211.2 121.8 all-reduce.14
  363.2 102.5 all-reduce.8
  496.9 102.5 all-reduce.10
  629.3 102.5 all-reduce.12
Sparse Core Ops, SparseCore 1:
  61.9 111.2 all-reduce.6
